TPU v7x, 32 devices: a whole 2x2x4 slice. The times are simulated.
32 devices in a mesh: dp: 8 (over z, y), head: 4 (over x, core).
Axes of the slice: x: 2, y: 2, z: 4, core: 2. Of those that a mesh axis runs over, the one named last changes fastest.
Arguments:
- tokens: float32 [64, 512, 768], P('dp', 'head'), may hold values from -6 to 6
- segment: int32 [64, 512], P('dp'), may hold values from 0 to 3, never falling along the last dimension, each value on 1 to 256 neighbouring positions
- modality: int32 [64, 512], P('dp', 'head'), may hold values from 0 to 1, as said below
- first_gain: float32 [2, 768], replicated, may hold values from 0.1 to 1.9
- first_shift: float32 [2, 768], replicated, may hold values from -1 to 1
- project_in: bfloat16 [768, 2304], replicated, may hold values from -0.21875 to 0.21875
- project_out: bfloat16 [768, 768], replicated, may hold values from -1.75 to 1.75
- second_gain: float32 [2, 768], replicated, may hold values from 0.1 to 1.9
- second_shift: float32 [2, 768], replicated, may hold values from -1 to 1
- up_weight: bfloat16 [2, 768, 3072], replicated, may hold values from -0.21875 to 0.21875
- down_weight: bfloat16 [2, 3072, 768], replicated, may hold values from -0.109375 to 0.109375
- cotangent: float32 [64, 512, 768], P('dp', 'head'), may hold values from -6 to 6
Outputs:
- output: float32 [64, 512, 768], P('dp', 'head')
- input_grad: float32 [64, 512, 768], P('dp', 'head')
- first_gain_grad: float32 [2, 768], P(None, 'dp')
- first_shift_grad: float32 [2, 768], P(None, 'dp')
- project_in_grad: float32 [768, 2304], P('dp')
- project_out_grad: float32 [768, 768], P('dp')
- second_gain_grad: float32 [2, 768], P(None, 'dp')
- second_shift_grad: float32 [2, 768], P(None, 'dp')
- up_weight_grad: float32 [2, 768, 3072], P(None, 'dp')
- down_weight_grad: float32 [2, 3072, 768], P(None, 'dp')
Inputs may be any that keep to these rules, and one draw needn't show every extreme that they name: Along each row segment numbers never fall; each segment is a run of 1 to 256 positions, and some run has exactly that many. On every device exactly 640 of its 1024 tokens have one modality and the others have the other one; which one is the larger varies by device.
All inputs are finite; a program needn't handle non-finite values.
Results may differ from a plain program's by a relative error of at most 0.015.
Values may be sent and summed in bfloat16 or wider, within the bound.
A program may use at most 320 MiB of HBM per device.

v0:
```python
import jax
import jax.numpy as jnp
from jax import lax
from jax.sharding import PartitionSpec as P

HEAD_DIM = 64
EXPERTS = 2
epsilon = 1e-05


def layer_norm(inputs, gains, shifts):
    centered = inputs - jnp.mean(inputs, axis=-1, keepdims=True)
    variance = jnp.mean(centered * centered, axis=-1, keepdims=True)
    return centered * lax.rsqrt(variance + epsilon) * gains + shifts


def pick(expert_table, token_kind):
    return jnp.where(token_kind[:, None] == 0, expert_table[0], expert_table[1])


def by_expert(per_token, token_kind):
    return jnp.stack(
        [
            jnp.sum(jnp.where(token_kind[:, None] == expert, per_token, 0.0), axis=0)
            for expert in range(EXPERTS)
        ]
    )


def gelu_exact(inputs):
    return jax.nn.gelu(inputs, approximate=False)


def body(
    tokens,
    segment,
    modality,
    first_gain,
    first_shift,
    project_in,
    project_out,
    second_gain,
    second_shift,
    up_weight,
    down_weight,
    cotangent,
):
    row_count, local_len, model_width = tokens.shape
    seq_len = segment.shape[1]
    token_count = row_count * local_len
    query_scale = HEAD_DIM ** (-0.5)
    flat_tokens = tokens.reshape(token_count, model_width)
    token_kind = modality.reshape(token_count)
    first_normed, first_back = jax.vjp(
        layer_norm, flat_tokens, pick(first_gain, token_kind), pick(first_shift, token_kind)
    )
    first_low = first_normed.astype(jnp.bfloat16)
    projected = jnp.dot(first_low, project_in, preferred_element_type=jnp.float32).astype(
        jnp.bfloat16
    )
    head_side = lax.all_to_all(
        projected.reshape(row_count, local_len, 3, model_width),
        "head",
        split_axis=3,
        concat_axis=1,
        tiled=True,
    )
    attend_rows = head_side.shape[0]
    heads_here = head_side.shape[3] // HEAD_DIM
    query = head_side[:, :, 0].reshape(attend_rows, seq_len, heads_here, HEAD_DIM) * query_scale
    keys = head_side[:, :, 1].reshape(attend_rows, seq_len, heads_here, HEAD_DIM)
    values = head_side[:, :, 2].reshape(attend_rows, seq_len, heads_here, HEAD_DIM)
    same_segment = (segment[:, :, None] == segment[:, None, :])[:, None]

    def masked_scores(query, keys):
        scores = jnp.einsum("rqhc,rkhc->rhqk", query, keys, preferred_element_type=jnp.float32)
        return jnp.where(same_segment, scores, -1000000000.0)

    masked = masked_scores(query, keys)
    peak = jnp.max(masked, axis=-1, keepdims=True)
    expanded = jnp.exp(masked - peak)
    totals = jnp.sum(expanded, axis=-1, keepdims=True)
    probs = expanded / totals
    log_total = peak + jnp.log(totals)
    context = jnp.einsum(
        "rhqk,rkhc->rqhc", probs.astype(jnp.bfloat16), values, preferred_element_type=jnp.float32
    )
    context = context.astype(jnp.bfloat16).reshape(attend_rows, seq_len, heads_here * HEAD_DIM)
    context_tok = lax.all_to_all(context, "head", split_axis=1, concat_axis=2, tiled=True)
    context_flat = context_tok.reshape(token_count, model_width)
    attention = jnp.dot(context_flat, project_out, preferred_element_type=jnp.float32)
    residual = flat_tokens + attention
    second_normed, second_back = jax.vjp(
        layer_norm, residual, pick(second_gain, token_kind), pick(second_shift, token_kind)
    )
    second_low = second_normed.astype(jnp.bfloat16)
    order = jnp.argsort(token_kind, stable=True)
    capacity = 5 * token_count // 8
    slot_sets = (order[:capacity], order[token_count - capacity :])
    branch_sum = jnp.zeros((token_count, model_width), jnp.float32)
    kept_items = []
    for expert in range(EXPERTS):
        slots = slot_sets[expert]
        live_rows = (token_kind[slots] == expert)[:, None]
        hidden = jnp.dot(second_low[slots], up_weight[expert], preferred_element_type=jnp.float32)
        activated, gelu_back = jax.vjp(gelu_exact, hidden)
        active_low = activated.astype(jnp.bfloat16)
        branch = jnp.dot(active_low, down_weight[expert], preferred_element_type=jnp.float32)
        branch_sum = branch_sum.at[slots].add(jnp.where(live_rows, branch, 0.0))
        kept_items.append((slots, live_rows, active_low, gelu_back))
    output = residual + branch_sum
    out_grad_flat = cotangent.reshape(token_count, model_width)
    grad_low = out_grad_flat.astype(jnp.bfloat16)
    second_grad = jnp.zeros((token_count, model_width), jnp.float32)
    up_terms = []
    down_terms = []
    for expert in range(EXPERTS):
        slots, live_rows, active_low, gelu_back = kept_items[expert]
        branch_grad = jnp.where(live_rows, grad_low[slots], jnp.zeros((), jnp.bfloat16))
        down_terms.append(
            jnp.einsum("tf,td->fd", active_low, branch_grad, preferred_element_type=jnp.float32)
        )
        active_grad = jnp.einsum(
            "td,fd->tf", branch_grad, down_weight[expert], preferred_element_type=jnp.float32
        )
        hidden_grad = gelu_back(active_grad)[0].astype(jnp.bfloat16)
        up_terms.append(
            jnp.einsum(
                "td,tf->df", second_low[slots], hidden_grad, preferred_element_type=jnp.float32
            )
        )
        second_grad = second_grad.at[slots].add(
            jnp.einsum(
                "tf,df->td", hidden_grad, up_weight[expert], preferred_element_type=jnp.float32
            )
        )
    residual_norm_grad, second_gain_tok, second_shift_tok = second_back(second_grad)
    second_gain_term = by_expert(second_gain_tok, token_kind)
    second_shift_term = by_expert(second_shift_tok, token_kind)
    up_term = jnp.stack(up_terms)
    down_term = jnp.stack(down_terms)
    residual_grad = out_grad_flat + residual_norm_grad
    attention_low = residual_grad.astype(jnp.bfloat16)
    out_term = jnp.einsum(
        "td,te->de", context_flat, attention_low, preferred_element_type=jnp.float32
    )
    context_grad = jnp.einsum(
        "te,de->td", attention_low, project_out, preferred_element_type=jnp.float32
    ).astype(jnp.bfloat16)
    context_grad = context_grad.reshape(row_count, local_len, model_width)
    context_heads = lax.all_to_all(context_grad, "head", split_axis=2, concat_axis=1, tiled=True)
    grad_heads = context_heads.reshape(attend_rows, seq_len, heads_here, HEAD_DIM)
    again = jnp.exp(masked_scores(query, keys) - log_total)
    prob_grad = jnp.einsum(
        "rqhc,rkhc->rhqk", grad_heads, values, preferred_element_type=jnp.float32
    )
    score_grad = (again * (prob_grad - jnp.sum(again * prob_grad, axis=-1, keepdims=True))).astype(
        jnp.bfloat16
    )
    query_grad = (
        jnp.einsum("rhqk,rkhc->rqhc", score_grad, keys, preferred_element_type=jnp.float32)
        * query_scale
    )
    keys_grad = jnp.einsum("rhqk,rqhc->rkhc", score_grad, query, preferred_element_type=jnp.float32)
    values_grad = jnp.einsum(
        "rhqk,rqhc->rkhc",
        again.astype(jnp.bfloat16),
        grad_heads,
        preferred_element_type=jnp.float32,
    )
    projected_grad = jnp.stack([query_grad, keys_grad, values_grad], axis=2).astype(jnp.bfloat16)
    projected_grad = projected_grad.reshape(attend_rows, seq_len, 3, heads_here * HEAD_DIM)
    grads_tok = lax.all_to_all(
        projected_grad, "head", split_axis=1, concat_axis=3, tiled=True
    ).reshape(token_count, 3 * model_width)
    first_grad = jnp.einsum("tf,df->td", grads_tok, project_in, preferred_element_type=jnp.float32)
    in_term = jnp.einsum("td,tf->df", first_low, grads_tok, preferred_element_type=jnp.float32)
    input_norm_grad, first_gain_tok, first_shift_tok = first_back(first_grad)
    input_grad = residual_grad + input_norm_grad
    first_gain_term = by_expert(first_gain_tok, token_kind)
    first_shift_term = by_expert(first_shift_tok, token_kind)
    weight_part = (
        lax.psum_scatter(first_gain_term, "dp", scatter_dimension=1, tiled=True),
        lax.psum_scatter(first_shift_term, "dp", scatter_dimension=1, tiled=True),
        lax.psum_scatter(in_term, "dp", scatter_dimension=0, tiled=True),
        lax.psum_scatter(out_term, "dp", scatter_dimension=0, tiled=True),
        lax.psum_scatter(second_gain_term, "dp", scatter_dimension=1, tiled=True),
        lax.psum_scatter(second_shift_term, "dp", scatter_dimension=1, tiled=True),
        lax.psum_scatter(up_term, "dp", scatter_dimension=1, tiled=True),
        lax.psum_scatter(down_term, "dp", scatter_dimension=1, tiled=True),
    )
    weight_sums = (
        lax.psum(weight_part[0].astype(jnp.bfloat16), "head").astype(jnp.float32),
        lax.psum(weight_part[1].astype(jnp.bfloat16), "head").astype(jnp.float32),
        lax.psum(weight_part[2].astype(jnp.bfloat16), "head").astype(jnp.float32),
        lax.psum(weight_part[3].astype(jnp.bfloat16), "head").astype(jnp.float32),
        lax.psum(weight_part[4].astype(jnp.bfloat16), "head").astype(jnp.float32),
        lax.psum(weight_part[5].astype(jnp.bfloat16), "head").astype(jnp.float32),
        lax.psum(weight_part[6].astype(jnp.bfloat16), "head").astype(jnp.float32),
        lax.psum(weight_part[7].astype(jnp.bfloat16), "head").astype(jnp.float32),
    )
    attention_sums = weight_sums[:4]
    expert_sums = weight_sums[4:]
    return (
        output.reshape(row_count, local_len, model_width),
        input_grad.reshape(row_count, local_len, model_width),
        attention_sums[0],
        attention_sums[1],
        attention_sums[2],
        attention_sums[3],
        expert_sums[0],
        expert_sums[1],
        expert_sums[2],
        expert_sums[3],
    )


def solution(mesh):
    return jax.shard_map(
        body,
        mesh=mesh,
        in_specs=(
            P("dp", "head", None),
            P("dp", None),
            P("dp", "head"),
            P(),
            P(),
            P(),
            P(),
            P(),
            P(),
            P(),
            P(),
            P("dp", "head", None),
        ),
        out_specs=(
            P("dp", "head", None),
            P("dp", "head", None),
            P(None, "dp"),
            P(None, "dp"),
            P("dp", None),
            P("dp", None),
            P(None, "dp"),
            P(None, "dp"),
            P(None, "dp", None),
            P(None, "dp", None),
        ),
        check_vma=False,
    )
```

profile of v0, /device:TPU:0, one launch (start us, length us, event | category | flops | bytes accessed | tf_op | source)
XLA Modules:
  0.0 1643.8 jit_solution(14196574063786381380)
XLA Ops:
  15.7 5.5 convolution_convert_fusion
  21.2 11.3 reshape.308
  32.5 7.6 copy.70
  40.1 5.1 all-to-all-start
  45.2 4.4 sort.17
  52.7 47.0 %all-to-all-done = bf16[8,128,3,768]{1,0,2,3:T(8,128)(2,1)} async-done(((bf16[8,128,3,768]{1,0,2,3:T(8,128)(2,1)}), bf16[8,128,3,768]{1,0,2,3:T(8,128)(2,1)}, u32[]{:S(2)}, u32[]{:S(2)}) %all-to-all-start) | async-done | bytes 4718624 | tf_op jit(solution)/shard_map/all_to_all | solution.py:61
  99.7 8.1 copy.72
  107.9 8.0 all_to_all.49
  118.9 10.5 select_reduce_fusion
  129.5 11.4 fusion
  140.9 12.4 fusion.62
  153.3 4.6 copy.74
  157.9 4.5 all-to-all-start.1
  163.0 4.5 gather_fusion.2
  170.6 5.5 gather_fusion.5
  176.2 4.5 gather_fusion
  180.6 5.5 gather_fusion.4
  196.2 4.4 fusion.96
  205.1 5.5 gather_fusion.3
  210.7 5.5 gather_fusion.1
  216.2 23.3 %multiply_convert_fusion.1 = (bf16[640,3072]{1,0:T(8,128)(2,1)}, f32[640,3072]{1,0:T(8,128)}, f32[640,3072]{1,0:T(8,128)}) fusion(bf16[640,768]{1,0:T(8,128)(2,1)} %gather_fusion.3, bf16[2,768,3072]{2,1,0:T(8,128)(2,1)} %param.21), kind=kOutput, calls=%fused_computation.31 | convolution fusion | flops 3147694080 | bytes 25362432 | tf_op jit(solution)/shard_map/dot_general | solution.py:105
  239.6 22.6 %multiply_convert_fusion.2 = (bf16[640,3072]{1,0:T(8,128)(2,1)}, f32[640,3072]{1,0:T(8,128)}, f32[640,3072]{1,0:T(8,128)}) fusion(bf16[640,768]{1,0:T(8,128)(2,1)S(1)} %copy-done.23, bf16[2,768,3072]{2,1,0:T(8,128)(2,1)} %param.21), kind=kOutput, calls=%fused_computation.44 | convolution fusion | flops 3147694080 | bytes 25362432 | tf_op jit(solution)/shard_map/dot_general | solution.py:105
  262.2 10.0 add_convert_fusion
  272.3 4.5 fusion.28
  276.8 9.9 add_convert_fusion.1
  288.6 4.6 fusion.36
  293.2 9.8 scatter_custom_fusion.2
  303.0 11.7 scatter_fusion
  314.7 5.2 select_reduce_fusion.4
  329.4 4.3 all-to-all-start.2
  335.3 5.2 fusion.66
  340.5 13.4 all-to-all-done.2
  361.8 19.9 %multiply_reduce_fusion = (f32[8,3,512]{2,1,0:T(4,128)S(1)}, f32[8,3,512,512]{2,3,1,0:T(8,128)}) fusion(f32[8,3,512,512]{2,3,1,0:T(8,128)} %get-tuple-element.56, f32[8,3,512]{2,1,0:T(4,128)} %log_add_fusion, pred[8,512,512]{1,2,0:T(8,128)(4,1)} %broadcast_compare_fusion, bf16[8,512,3,64]{1,3,2,0:T(8,128)(2,1)} %reshape.215, ...), kind=kOutput, calls=%fused_computation.11 | convolution fusion | flops 830459904 | bytes 55672832 | tf_op jit(solution)/shard_map/rqhc,rkhc->rhqk/dot_general | solution.py:154
  381.7 17.6 %multiply_convert_fusion = bf16[8,3,512,512]{2,3,1,0:T(8,128)(2,1)S(1)} fusion(f32[8,3,512,512]{2,3,1,0:T(8,128)} %get-tuple-element.62, f32[8,3,512,512]{2,3,1,0:T(8,128)} %get-tuple-element.56, f32[8,3,512]{2,1,0:T(4,128)S(1)} %get-tuple-element.61, f32[8,3,512]{2,1,0:T(4,128)S(1)} %copy-done.31, pred[8,512,512]{1,2,0:T(8,128)(4,1)S(1)} %copy-done.7), kind=kLoop, calls=%fused_computation.10 | loop fusion | flops 31457280 | bytes 65110016 | tf_op jit(solution)/shard_map/convert_element_type | solution.py:157
  399.3 4.6 copy-done.4
  407.2 9.8 convolution_convert_fusion.1
  417.1 13.1 fusion.63
  430.2 4.4 copy.83
  434.6 4.4 copy.84
  439.1 4.4 copy.85
  443.5 6.7 pad_maximum_fusion.2
  450.2 5.2 all-to-all-start.3
  459.1 67.0 %all-to-all-done.3 = bf16[8,512,3,192]{3,0,2,1:T(8,128)(2,1)} async-done(((bf16[8,512,3,192]{3,0,2,1:T(8,128)(2,1)}), bf16[8,512,3,192]{3,0,2,1:T(8,128)(2,1)}, u32[]{:S(2)}, u32[]{:S(2)}) %all-to-all-start.3) | async-done | bytes 4718624 | tf_op jit(solution)/shard_map/all_to_all | solution.py:173
  526.1 8.6 copy.97
  534.7 5.5 copy.87
  542.4 5.9 fusion.20
  548.6 6.4 convolution_bitcast_fusion.2
  559.0 7.0 pad_maximum_fusion
  566.6 6.5 convolution_bitcast_fusion
  577.2 6.9 pad_maximum_fusion.1
  593.9 11.0 select_reduce_fusion.8
  612.9 8.2 fusion.34
  622.7 56.0 %reduce-scatter.17.cloned.1.call-done = f32[96,2304]{1,0:T(8,128)} async-done(((f32[768,2304]{1,0:T(8,128)}), f32[96,2304]{1,0:T(8,128)}) %reduce-scatter.17.cloned.1.call-update) | async-done | bytes 884752 | tf_op jit(solution)/shard_map/reduce_scatter | solution.py:185
  680.6 310.8 %reduce-scatter.21.cloned.1.call-done = f32[2,96,3072]{2,1,0:T(8,128)} async-done(((f32[2,768,3072]{2,1,0:T(8,128)}), f32[2,96,3072]{2,1,0:T(8,128)}) %reduce-scatter.21.cloned.1.call-update) | async-done | bytes 2359312 | tf_op jit(solution)/shard_map/reduce_scatter | solution.py:189
  994.2 309.7 %reduce-scatter.23.cloned.1.call-done = f32[2,384,768]{2,1,0:T(8,128)} async-done(((f32[2,3072,768]{2,1,0:T(8,128)}), f32[2,384,768]{2,1,0:T(8,128)}) %reduce-scatter.23.cloned.1.call-update) | async-done | bytes 2359312 | tf_op jit(solution)/shard_map/reduce_scatter | solution.py:190
  1306.8 8.0 fusion.26
  1314.8 12.2 scatter_custom_fusion
  1327.0 12.1 scatter_custom_fusion.1
  1339.1 29.3 %reduce-scatter.31.cloned.1.call-done = f32[96,2]{1,0:T(8,128)} async-done(((f32[768,2]{1,0:T(8,128)}), f32[96,2]{1,0:T(8,128)}) %reduce-scatter.31.cloned.1.call-update) | async-done | bytes 784
  1369.8 63.0 %reduce-scatter.29.cloned.1.call-done = f32[96,2]{1,0:T(8,128)} async-done(((f32[768,2]{1,0:T(8,128)}), f32[96,2]{1,0:T(8,128)}) %reduce-scatter.29.cloned.1.call-update) | async-done | bytes 784
  1440.9 56.5 %reduce-scatter.27.cloned.1.call-done = f32[96,2]{1,0:T(8,128)} async-done(((f32[768,2]{1,0:T(8,128)}), f32[96,2]{1,0:T(8,128)}) %reduce-scatter.27.cloned.1.call-update) | async-done | bytes 784
  1498.3 63.7 %reduce-scatter.25.cloned.1.call-done = f32[96,2]{1,0:T(8,128)} async-done(((f32[768,2]{1,0:T(8,128)}), f32[96,2]{1,0:T(8,128)}) %reduce-scatter.25.cloned.1.call-update) | async-done | bytes 784
  1562.9 6.2 all-reduce
  1574.0 55.6 %all-reduce.4.cloned.1.call-done = (bf16[96,2304]{1,0:T(8,128)(2,1)}, bf16[96,768]{1,0:T(8,128)(2,1)}, bf16[2,96,3072]{2,1,0:T(8,128)(2,1)}, bf16[2,384,768]{2,1,0:T(8,128)(2,1)}) async-done(((bf16[96,2304]{1,0:T(8,128)(2,1)}, bf16[96,768]{1,0:T(8,128)(2,1)}, bf16[2,96,3072]{2,1,0:T(8,128)(2,1)}, bf16[2,384,768]{2,1,0:T(8,128)(2,1)}), (bf16[96,2304]{1,0:T(8,128)(2,1)}, bf16[96,768]{1,0:T(8,128)(2,1)}, ...) | async-done | bytes 2949136 | tf_op jit(solution)/shard_map/psum | solution.py:195
  (245 shorter events, 122.1 us)
Async XLA Ops:
  7.2 8.5 copy-start
  7.2 4.9 copy-start.1
  7.2 5.4 copy-start.64
  9.5 4.6 copy-start.5
  40.1 59.6 %all-to-all-start = ((bf16[8,128,3,768]{1,0,2,3:T(8,128)(2,1)}), bf16[8,128,3,768]{1,0,2,3:T(8,128)(2,1)}, u32[]{:S(2)}, u32[]{:S(2)}) async-start(bf16[8,128,3,768]{1,0,2,3:T(8,128)(2,1)} %copy.70), calls=%async_computation | async-start | bytes 9437184 | tf_op jit(solution)/shard_map/all_to_all | solution.py:61
  118.7 10.7 copy-start.10
  118.7 10.7 copy-start.12
  118.7 22.1 %copy-start.17 = (bf16[8,512,1,192]{1,3,2,0:T(8,128)(2,1)}, bf16[8,512,1,192]{1,3,2,0:T(8,128)(2,1)S(1)}, u32[]{:S(2)}) copy-start(bf16[8,512,1,192]{1,3,2,0:T(8,128)(2,1)S(1)} %get-tuple-element.48) | copy-start | bytes 4718596
  129.5 11.4 copy-start.30
  140.9 12.4 copy-start.33
  157.9 32.2 %all-to-all-start.1 = ((bf16[8,512,192]{2,0,1:T(8,128)(2,1)}), bf16[8,512,192]{2,0,1:T(8,128)(2,1)}, u32[]{:S(2)}, u32[]{:S(2)}) async-start(bf16[8,512,192]{2,0,1:T(8,128)(2,1)} %copy.74), calls=%async_computation.1 | async-start | bytes 4194304 | tf_op jit(solution)/shard_map/all_to_all | solution.py:89
  162.4 13.8 copy-start.51
  187.6 14.7 copy-start.39
  187.6 14.7 copy-start.41
  196.2 6.6 copy-start.59
  196.2 6.6 copy-start.62
  196.2 6.6 copy-start.63
  216.2 23.4 %copy-start.23 = (bf16[640,768]{1,0:T(8,128)(2,1)S(1)}, bf16[640,768]{1,0:T(8,128)(2,1)}, u32[]{:S(2)}) copy-start(bf16[640,768]{1,0:T(8,128)(2,1)} %gather_fusion.1) | copy-start | bytes 2949124
  216.2 56.0 %slice-start = ((s8[9437184]{0:T(1024)(128)(4,1)}), s8[4194304]{0:T(1024)(128)(4,1)S(1)}, s32[]{:S(2)}) async-start(s8[9437184]{0:T(1024)(128)(4,1)} %bitcast.193), calls=%async_computation.21 | async-start | bytes 8388608
  216.2 56.0 %slice-start.1 = ((s8[9437184]{0:T(1024)(128)(4,1)}), s8[4194304]{0:T(1024)(128)(4,1)S(1)}, s32[]{:S(2)}) async-start(s8[9437184]{0:T(1024)(128)(4,1)} %bitcast.193), calls=%async_computation.22 | async-start | bytes 8388608
  239.6 22.6 %copy-start.27 = (bf16[640,768]{1,0:T(8,128)(2,1)S(1)}, bf16[640,768]{1,0:T(8,128)(2,1)}, u32[]{:S(2)}) copy-start(bf16[640,768]{1,0:T(8,128)(2,1)} %gather_fusion.5) | copy-start | bytes 2949124
  239.6 22.6 %copy-start.65 = (pred[640]{0:T(1024)(128)(4,1)S(1)}, pred[640]{0:T(1024)(128)(4,1)}, u32[]{:S(2)}) copy-start(pred[640]{0:T(1024)(128)(4,1)} %broadcast_compare_fusion.3) | copy-start | bytes 1924
  239.6 32.7 %slice-start.2 = ((s8[9437184]{0:T(1024)(128)(4,1)}), s8[1048576]{0:T(1024)(128)(4,1)S(1)}, s32[]{:S(2)}) async-start(s8[9437184]{0:T(1024)(128)(4,1)} %bitcast.193), calls=%async_computation.23 | async-start | bytes 2097152
  272.3 4.6 copy-start.20
  272.3 4.6 copy-start.28
  303.0 11.7 copy-start.36
  303.0 11.7 copy-start.40
  303.0 11.7 copy-start.42
  303.0 11.7 copy-start.44
  314.6 5.2 copy-start.50
  314.6 5.2 copy-start.3
  314.7 5.3 copy-start.9
  314.7 5.3 copy-start.60
  329.4 24.5 %all-to-all-start.2 = ((bf16[8,128,768]{1,0,2:T(8,128)(2,1)}), bf16[8,128,768]{1,0,2:T(8,128)(2,1)}, u32[]{:S(2)}, u32[]{:S(2)}) async-start(bf16[8,128,768]{1,0,2:T(8,128)(2,1)} %copy.77), calls=%async_computation.2 | async-start | bytes 3145728 | tf_op jit(solution)/shard_map/all_to_all | solution.py:151
  333.7 287.3 %reduce-scatter.19.cloned.1.call-start = ((), (), s32[]{:S(2)}) async-start(), calls=%async_computation.13 | async-start | bytes 2654208 | tf_op jit(solution)/shard_map/reduce_scatter | solution.py:186
  361.8 19.9 %copy-start.7 = (pred[8,512,512]{1,2,0:T(8,128)(4,1)S(1)}, pred[8,512,512]{1,2,0:T(8,128)(4,1)}, u32[]{:S(2)}) copy-start(pred[8,512,512]{1,2,0:T(8,128)(4,1)} %broadcast_compare_fusion) | copy-start | bytes 6291460
  361.8 19.9 %copy-start.31 = (f32[8,3,512]{2,1,0:T(4,128)S(1)}, f32[8,3,512]{2,1,0:T(4,128)}, u32[]{:S(2)}) copy-start(f32[8,3,512]{2,1,0:T(4,128)} %log_add_fusion) | copy-start | bytes 147460
  381.7 22.2 %copy-start.13 = (bf16[8,512,1,192]{1,3,2,0:T(8,128)(2,1)S(1)}, bf16[8,512,1,192]{1,3,2,0:T(8,128)(2,1)}, u32[]{:S(2)}) copy-start(bf16[8,512,1,192]{1,3,2,0:T(8,128)(2,1)} %copy-done.12) | copy-start | bytes 4718596
  399.3 4.6 copy-start.4
  407.2 9.9 copy-start.18
  450.2 5.3 copy-start.2
  450.2 5.3 copy-start.38
  450.2 5.4 copy-start.46
  450.2 5.4 copy-start.48
  450.2 75.9 %all-to-all-start.3 = ((bf16[8,512,3,192]{3,0,2,1:T(8,128)(2,1)}), bf16[8,512,3,192]{3,0,2,1:T(8,128)(2,1)}, u32[]{:S(2)}, u32[]{:S(2)}) async-start(bf16[8,512,3,192]{3,0,2,1:T(8,128)(2,1)} %pad_maximum_fusion.2), calls=%async_computation.3 | async-start | bytes 12582912 | tf_op jit(solution)/shard_map/all_to_all | solution.py:173
  455.5 223.2 %reduce-scatter.17.cloned.1.call-start = ((), (), s32[]{:S(2)}) async-start(), calls=%async_computation.12 | async-start | bytes 7962624 | tf_op jit(solution)/shard_map/reduce_scatter | solution.py:185
  534.7 7.7 copy-start.26
  548.3 443.1 %reduce-scatter.21.cloned.1.call-start = ((), (), s32[]{:S(2)}) async-start(), calls=%async_computation.14 | async-start | bytes 21233664 | tf_op jit(solution)/shard_map/reduce_scatter | solution.py:189
  548.6 6.5 copy-start.22
  548.6 6.5 copy-start.24
  566.0 738.0 %reduce-scatter.23.cloned.1.call-start = ((), (), s32[]{:S(2)}) async-start(), calls=%async_computation.15 | async-start | bytes 21233664 | tf_op jit(solution)/shard_map/reduce_scatter | solution.py:190
  566.6 6.5 copy-start.29
  566.6 6.5 copy-start.68
  566.6 6.5 copy-start.72
  584.1 9.8 copy-start.53
  584.1 784.3 %reduce-scatter.31.cloned.1.call-start = ((), (), s32[]{:S(2)}) async-start(), calls=%async_computation.19 | async-start | bytes 442368
  590.3 842.5 %reduce-scatter.29.cloned.1.call-start = ((), (), s32[]{:S(2)}) async-start(), calls=%async_computation.18 | async-start | bytes 442368
  593.4 904.1 %reduce-scatter.27.cloned.1.call-start = ((), (), s32[]{:S(2)}) async-start(), calls=%async_computation.17 | async-start | bytes 442368
  609.7 952.3 %reduce-scatter.25.cloned.1.call-start = ((), (), s32[]{:S(2)}) async-start(), calls=%async_computation.16 | async-start | bytes 442368
  612.7 1016.9 %all-reduce.4.cloned.1.call-start = ((), (), s32[]{:S(2)}) async-start(), calls=%async_computation.20 | async-start | bytes 5898240 | tf_op jit(solution)/shard_map/psum | solution.py:195
  1438.9 124.0 %copy-start.69 = (bf16[2,96]{1,0:T(2,128)(2,1)S(1)}, bf16[2,96]{1,0:T(2,128)(2,1)}, u32[]{:S(2)}) copy-start(bf16[2,96]{1,0:T(2,128)(2,1)} %copy.105) | copy-start | bytes 1156
  1438.9 124.0 %copy-start.70 = (bf16[2,96]{1,0:T(2,128)(2,1)S(1)}, bf16[2,96]{1,0:T(2,128)(2,1)}, u32[]{:S(2)}) copy-start(bf16[2,96]{1,0:T(2,128)(2,1)} %copy.103) | copy-start | bytes 1156
  1629.5 5.8 copy-start.32
  1629.5 6.8 copy-start.34
  (25 other events, 49.3 us)
Sparse Core Ops, SparseCore 0:
  340.6 72.0 reduce-scatter.18
  548.4 130.1 reduce-scatter.16
  682.5 308.8 reduce-scatter.20
  995.1 308.8 reduce-scatter.22
  1307.1 61.3 reduce-scatter.30
  1371.6 61.2 reduce-scatter.28
  1436.1 61.2 reduce-scatter.26
  1500.7 61.2 reduce-scatter.24
  1565.2 64.3 all-reduce.3
where the time goes:
time: 1650 us; the launch traced here: 1640 us
  waiting for transfers between devices  1070 us (65%)
  matrix products  216 us (13%)
  other arithmetic  166 us (10%)
  local copies, waits for them, and re-layouts  149 us (9%)
  starting transfers between devices  20.7 us (1%)
    reduce_scatter x1, waiting for transfers between devices, body(): lax.psum_scatter(up_term, 'dp', scatter_dimension=1, tiled=True)  311 us
    reduce_scatter x1, waiting for transfers between devices, body(): lax.psum_scatter(down_term, 'dp', scatter_dimension=1, tiled=True)  310 us
    unnamed x13, waiting for transfers between devices  213 us
    all_to_all x1, waiting for transfers between devices, body(): lax.all_to_all(projected_grad, 'head', split_axis=1, concat_axis=3, tiled...  67 us
    reduce_scatter x1, waiting for transfers between devices, body(): lax.psum_scatter(in_term, 'dp', scatter_dimension=0, tiled=True)  56 us
    psum x1, waiting for transfers between devices, body(): lax.psum(weight_part[2].astype(jnp.bfloat16), 'head').astype(jnp.float32)  55.6 us
    all_to_all x1, waiting for transfers between devices, body(): lax.all_to_all(projected.reshape(row_count, local_len, 3, model_width), '...  47 us
    dot_general x2, matrix products, body(): jnp.dot(second_low[slots], up_weight[expert], preferred_element_type=jnp....  45.9 us
  transfers between devices with their start and end apart: 13, of which 11 were waited for; matrix products, arithmetic and copies ran while one was open for 17% of the time, Pallas kernels for 0%

commit v1 on v0

--- a/solution.py
+++ b/solution.py
@@ -1,3 +1,4 @@
+import functools
 import jax
 import jax.numpy as jnp
 from jax import lax
@@ -6,6 +7,36 @@
 HEAD_DIM = 64
 EXPERTS = 2
 epsilon = 1e-05
+
+
+def settle_files(page, on_dim, block_here):
+    shaped, opened = (page.shape[:on_dim], page.shape[on_dim + 1 :])
+    raw_out = jnp.moveaxis(page.reshape(*shaped, block_here, -1, *opened), on_dim, 0)
+    return raw_out
+
+
+def kinds_settle(my_data, dim_no):
+    far_arr = list(my_data.shape[1:])
+    far_arr[dim_no] *= my_data.shape[0]
+    kept_arr = jnp.moveaxis(my_data, 0, dim_no).reshape(far_arr)
+    return kept_arr
+
+
+def choose_the_tokens(vals, link_axis, packet, local_x):
+    w1, o_now = (jax.lax.axis_size(link_axis), jax.lax.axis_index(link_axis))
+    v_now = settle_files(vals, packet, w1)
+    chunks = [v_now[o_now]]
+    j0 = 1
+    while j0 < w1:
+        odd = v_now[o_now ^ j0]
+        chunks.append(jax.lax.ppermute(odd, link_axis, [(w, w ^ j0) for w in range(w1)]))
+        j0 += 1
+    v_now = jnp.stack(chunks)[o_now ^ jnp.arange(w1)]
+    reply = kinds_settle(v_now, local_x)
+    return reply
+
+
+tell_the_leaves = functools.partial(choose_the_tokens, link_axis="head", packet=3, local_x=1)
 
 
 def layer_norm(inputs, gains, shifts):
@@ -58,13 +89,7 @@
     projected = jnp.dot(first_low, project_in, preferred_element_type=jnp.float32).astype(
         jnp.bfloat16
     )
-    head_side = lax.all_to_all(
-        projected.reshape(row_count, local_len, 3, model_width),
-        "head",
-        split_axis=3,
-        concat_axis=1,
-        tiled=True,
-    )
+    head_side = tell_the_leaves(projected.reshape(row_count, local_len, 3, model_width))
     attend_rows = head_side.shape[0]
     heads_here = head_side.shape[3] // HEAD_DIM
     query = head_side[:, :, 0].reshape(attend_rows, seq_len, heads_here, HEAD_DIM) * query_scale

time: 1650 us -> 1640 us (level)
    all_to_all x1 -> x0, waiting for transfers between devices: 47 us -> none  [body(): lax.all_to_all(projected.reshape(row_count, local_len, 3, model_width), '...]
    ppermute x0 -> x3, waiting for transfers between devices: none -> 40 us  [choose_the_tokens(): jax.lax.ppermute(odd, link_axis, [(w, w ^ j0) for w in range(w1)])]
  transfers between devices with their start and end apart: 13 -> 15, of which waited for: 11 -> 12; matrix products, arithmetic and copies ran while one was open for 17% -> 18% of each run, Pallas kernels for 0% -> 0%
where the time goes in v1:
time: 1640 us; the launch traced here: 1630 us
  waiting for transfers between devices  1060 us (65%)
  matrix products  216 us (13%)
  other arithmetic  167 us (10%)
  local copies, waits for them, and re-layouts  144 us (9%)
  starting transfers between devices  18.7 us (1%)
    reduce_scatter x1, waiting for transfers between devices, body(): lax.psum_scatter(up_term, 'dp', scatter_dimension=1, tiled=True)  311 us
    reduce_scatter x1, waiting for transfers between devices, body(): lax.psum_scatter(down_term, 'dp', scatter_dimension=1, tiled=True)  310 us
    unnamed x13, waiting for transfers between devices  213 us
    all_to_all x1, waiting for transfers between devices, body(): lax.all_to_all(projected_grad, 'head', split_axis=1, concat_axis=3, tiled...  67 us
    reduce_scatter x1, waiting for transfers between devices, body(): lax.psum_scatter(in_term, 'dp', scatter_dimension=0, tiled=True)  55.8 us
    psum x1, waiting for transfers between devices, body(): lax.psum(weight_part[2].astype(jnp.bfloat16), 'head').astype(jnp.float32)  55.6 us
    dot_general x2, matrix products, body(): jnp.dot(second_low[slots], up_weight[expert], preferred_element_type=jnp....  46.1 us
    ppermute x3, waiting for transfers between devices, choose_the_tokens(): jax.lax.ppermute(odd, link_axis, [(w, w ^ j0) for w in range(w1)])  40 us
  transfers between devices with their start and end apart: 15, of which 12 were waited for; matrix products, arithmetic and copies ran while one was open for 18% of the time, Pallas kernels for 0%

profile of v1, /device:TPU:0, one launch (start us, length us, event | category | flops | bytes accessed | tf_op | source)
XLA Modules:
  0.0 1631.8 jit_solution(4828476635316545702)
XLA Ops:
  15.7 5.5 convolution_convert_fusion
  21.2 6.6 copy.76
  27.9 5.7 copy.113
  44.5 4.4 sort.17
  52.0 14.6 collective-permute-done.2
  66.6 25.4 %collective-permute-done.1 = bf16[8,128,3,192]{1,3,2,0:T(8,128)(2,1)} collective-permute-done((bf16[8,128,3,192]{1,3,2,0:T(8,128)(2,1)}, bf16[8,128,3,192]{1,3,2,0:T(8,128)(2,1)}, u32[]{:S(2)}, u32[]{:S(2)}) %collective-permute-start.1) | collective-permute-done | bytes 1179680 | tf_op jit(solution)/shard_map/ppermute | solution.py:32
  96.0 5.6 gather_fusion
  107.0 10.6 select_reduce_fusion
  117.6 11.4 fusion
  129.0 12.6 fusion.62
  141.6 4.4 copy.83
  145.9 4.5 all-to-all-start
  151.1 4.5 gather_fusion.3
  158.7 5.5 gather_fusion.6
  164.2 4.5 gather_fusion.1
  168.7 5.5 gather_fusion.5
  184.3 4.4 fusion.97
  193.2 5.5 gather_fusion.4
  198.8 5.5 gather_fusion.2
  204.3 23.4 %multiply_convert_fusion.1 = (bf16[640,3072]{1,0:T(8,128)(2,1)}, f32[640,3072]{1,0:T(8,128)}, f32[640,3072]{1,0:T(8,128)}) fusion(bf16[640,768]{1,0:T(8,128)(2,1)} %gather_fusion.4, bf16[2,768,3072]{2,1,0:T(8,128)(2,1)} %param.21), kind=kOutput, calls=%fused_computation.32 | convolution fusion | flops 3147694080 | bytes 25362432 | tf_op jit(solution)/shard_map/dot_general | solution.py:130
  227.7 22.7 %multiply_convert_fusion.2 = (bf16[640,3072]{1,0:T(8,128)(2,1)}, f32[640,3072]{1,0:T(8,128)}, f32[640,3072]{1,0:T(8,128)}) fusion(bf16[640,768]{1,0:T(8,128)(2,1)S(1)} %copy-done.23, bf16[2,768,3072]{2,1,0:T(8,128)(2,1)} %param.21), kind=kOutput, calls=%fused_computation.45 | convolution fusion | flops 3147694080 | bytes 25362432 | tf_op jit(solution)/shard_map/dot_general | solution.py:130
  250.4 10.0 add_convert_fusion
  260.5 4.6 fusion.28
  265.1 9.9 add_convert_fusion.1
  276.9 4.6 fusion.36
  281.4 9.8 scatter_custom_fusion.2
  291.2 11.7 scatter_fusion
  303.0 5.2 select_reduce_fusion.4
  317.6 4.4 all-to-all-start.1
  323.6 5.2 fusion.66
  328.7 13.5 all-to-all-done.1
  346.1 4.1 reshape.238
  350.2 20.0 %multiply_reduce_fusion = (f32[8,3,512]{2,1,0:T(4,128)S(1)}, f32[8,3,512,512]{2,3,1,0:T(8,128)}) fusion(f32[8,3,512,512]{2,3,1,0:T(8,128)} %get-tuple-element.60, f32[8,3,512]{2,1,0:T(4,128)} %log_add_fusion, pred[8,512,512]{1,2,0:T(8,128)(4,1)} %broadcast_compare_fusion, bf16[8,512,3,64]{1,3,2,0:T(8,128)(2,1)} %reshape.238, ...), kind=kOutput, calls=%fused_computation.12 | convolution fusion | flops 830459904 | bytes 55672832 | tf_op jit(solution)/shard_map/rqhc,rkhc->rhqk/dot_general | solution.py:179
  370.2 17.6 %multiply_convert_fusion = bf16[8,3,512,512]{2,3,1,0:T(8,128)(2,1)S(1)} fusion(f32[8,3,512,512]{2,3,1,0:T(8,128)} %get-tuple-element.66, f32[8,3,512,512]{2,3,1,0:T(8,128)} %get-tuple-element.60, f32[8,3,512]{2,1,0:T(4,128)S(1)} %get-tuple-element.65, f32[8,3,512]{2,1,0:T(4,128)S(1)} %copy-done.31, pred[8,512,512]{1,2,0:T(8,128)(4,1)S(1)} %copy-done.7), kind=kLoop, calls=%fused_computation.11 | loop fusion | flops 31457280 | bytes 65110016 | tf_op jit(solution)/shard_map/convert_element_type | solution.py:182
  387.8 4.6 copy-done.4
  395.7 9.8 convolution_convert_fusion.1
  405.6 13.1 fusion.63
  418.7 4.4 copy.92
  423.1 4.4 copy.93
  427.5 4.4 copy.94
  431.9 6.7 pad_maximum_fusion.2
  438.7 5.2 all-to-all-start.2
  447.6 67.0 %all-to-all-done.2 = bf16[8,512,3,192]{3,0,2,1:T(8,128)(2,1)} async-done(((bf16[8,512,3,192]{3,0,2,1:T(8,128)(2,1)}), bf16[8,512,3,192]{3,0,2,1:T(8,128)(2,1)}, u32[]{:S(2)}, u32[]{:S(2)}) %all-to-all-start.2) | async-done | bytes 4718624 | tf_op jit(solution)/shard_map/all_to_all | solution.py:198
  514.6 8.6 copy.103
  523.2 5.5 copy.96
  530.8 5.9 fusion.20
  537.0 6.4 convolution_bitcast_fusion.2
  547.4 6.9 pad_maximum_fusion
  555.0 6.5 convolution_bitcast_fusion
  565.6 6.9 pad_maximum_fusion.1
  582.3 11.0 select_reduce_fusion.8
  601.3 8.2 fusion.34
  611.1 55.8 %reduce-scatter.17.cloned.1.call-done = f32[96,2304]{1,0:T(8,128)} async-done(((f32[768,2304]{1,0:T(8,128)}), f32[96,2304]{1,0:T(8,128)}) %reduce-scatter.17.cloned.1.call-update) | async-done | bytes 884752 | tf_op jit(solution)/shard_map/reduce_scatter | solution.py:210
  668.8 310.7 %reduce-scatter.21.cloned.1.call-done = f32[2,96,3072]{2,1,0:T(8,128)} async-done(((f32[2,768,3072]{2,1,0:T(8,128)}), f32[2,96,3072]{2,1,0:T(8,128)}) %reduce-scatter.21.cloned.1.call-update) | async-done | bytes 2359312 | tf_op jit(solution)/shard_map/reduce_scatter | solution.py:214
  982.4 309.7 %reduce-scatter.23.cloned.1.call-done = f32[2,384,768]{2,1,0:T(8,128)} async-done(((f32[2,3072,768]{2,1,0:T(8,128)}), f32[2,384,768]{2,1,0:T(8,128)}) %reduce-scatter.23.cloned.1.call-update) | async-done | bytes 2359312 | tf_op jit(solution)/shard_map/reduce_scatter | solution.py:215
  1294.9 8.0 fusion.26
  1302.9 12.2 scatter_custom_fusion
  1315.2 12.1 scatter_custom_fusion.1
  1327.2 29.3 %reduce-scatter.31.cloned.1.call-done = f32[96,2]{1,0:T(8,128)} async-done(((f32[768,2]{1,0:T(8,128)}), f32[96,2]{1,0:T(8,128)}) %reduce-scatter.31.cloned.1.call-update) | async-done | bytes 784
  1357.9 63.0 %reduce-scatter.29.cloned.1.call-done = f32[96,2]{1,0:T(8,128)} async-done(((f32[768,2]{1,0:T(8,128)}), f32[96,2]{1,0:T(8,128)}) %reduce-scatter.29.cloned.1.call-update) | async-done | bytes 784
  1428.9 56.4 %reduce-scatter.27.cloned.1.call-done = f32[96,2]{1,0:T(8,128)} async-done(((f32[768,2]{1,0:T(8,128)}), f32[96,2]{1,0:T(8,128)}) %reduce-scatter.27.cloned.1.call-update) | async-done | bytes 784
  1486.2 63.7 %reduce-scatter.25.cloned.1.call-done = f32[96,2]{1,0:T(8,128)} async-done(((f32[768,2]{1,0:T(8,128)}), f32[96,2]{1,0:T(8,128)}) %reduce-scatter.25.cloned.1.call-update) | async-done | bytes 784
  1550.8 6.2 all-reduce
  1561.9 55.6 %all-reduce.4.cloned.1.call-done = (bf16[96,2304]{1,0:T(8,128)(2,1)}, bf16[96,768]{1,0:T(8,128)(2,1)}, bf16[2,96,3072]{2,1,0:T(8,128)(2,1)}, bf16[2,384,768]{2,1,0:T(8,128)(2,1)}) async-done(((bf16[96,2304]{1,0:T(8,128)(2,1)}, bf16[96,768]{1,0:T(8,128)(2,1)}, bf16[2,96,3072]{2,1,0:T(8,128)(2,1)}, bf16[2,384,768]{2,1,0:T(8,128)(2,1)}), (bf16[96,2304]{1,0:T(8,128)(2,1)}, bf16[96,768]{1,0:T(8,128)(2,1)}, ...) | async-done | bytes 2949136 | tf_op jit(solution)/shard_map/psum | solution.py:220
  (257 shorter events, 135.2 us)
Async XLA Ops:
  7.2 8.5 copy-start
  7.2 4.9 copy-start.1
  7.2 5.4 copy-start.64
  37.5 29.1 %collective-permute-start.2 = (bf16[8,128,3,192]{1,3,2,0:T(8,128)(2,1)}, bf16[8,128,3,192]{1,3,2,0:T(8,128)(2,1)}, u32[]{:S(2)}, u32[]{:S(2)}) collective-permute-start(bf16[8,128,3,192]{1,3,2,0:T(8,128)(2,1)} %bitcast.181), channel_id=1, source_target_pairs={{0,3},{1,2},{2,1},{3,0},{4,7},{5,6},{6,5},{7,4},{8,11},{9,10},{10,... | collective-permute-start | bytes 3538952 | tf_op jit(solution)/shard_map/ppermute | solution.py:32
  41.2 25.4 %collective-permute-start = (bf16[8,128,3,192]{1,3,2,0:T(8,128)(2,1)}, bf16[8,128,3,192]{1,3,2,0:T(8,128)(2,1)}, u32[]{:S(2)}, u32[]{:S(2)}) collective-permute-start(bf16[8,128,3,192]{1,3,2,0:T(8,128)(2,1)} %bitcast.183), channel_id=1, source_target_pairs={{0,1},{1,0},{2,3},{3,2},{4,5},{5,4},{6,7},{7,6},{8,9},{9,8},{10,11... | collective-permute-start | bytes 3538952 | tf_op jit(solution)/shard_map/ppermute | solution.py:32
  43.1 48.9 %collective-permute-start.1 = (bf16[8,128,3,192]{1,3,2,0:T(8,128)(2,1)}, bf16[8,128,3,192]{1,3,2,0:T(8,128)(2,1)}, u32[]{:S(2)}, u32[]{:S(2)}) collective-permute-start(bf16[8,128,3,192]{1,3,2,0:T(8,128)(2,1)} %bitcast.182), channel_id=1, source_target_pairs={{0,2},{1,3},{2,0},{3,1},{4,6},{5,7},{6,4},{7,5},{8,10},{9,11},{10,... | collective-permute-start | bytes 3538952 | tf_op jit(solution)/shard_map/ppermute | solution.py:32
  105.0 12.6 copy-start.10
  105.0 12.6 copy-start.12
  105.0 24.0 %copy-start.17 = (bf16[8,512,1,192]{1,3,2,0:T(8,128)(2,1)}, bf16[8,512,1,192]{1,3,2,0:T(8,128)(2,1)S(1)}, u32[]{:S(2)}) copy-start(bf16[8,512,1,192]{1,3,2,0:T(8,128)(2,1)S(1)} %get-tuple-element.48) | copy-start | bytes 4718596
  117.6 11.4 copy-start.30
  129.0 12.6 copy-start.33
  145.9 32.2 %all-to-all-start = ((bf16[8,512,192]{2,0,1:T(8,128)(2,1)}), bf16[8,512,192]{2,0,1:T(8,128)(2,1)}, u32[]{:S(2)}, u32[]{:S(2)}) async-start(bf16[8,512,192]{2,0,1:T(8,128)(2,1)} %copy.83), calls=%async_computation | async-start | bytes 4194304 | tf_op jit(solution)/shard_map/all_to_all | solution.py:114
  150.5 13.8 copy-start.51
  175.6 14.6 copy-start.39
  175.6 14.6 copy-start.41
  184.3 6.6 copy-start.59
  184.3 6.6 copy-start.62
  184.3 6.6 copy-start.63
  204.3 23.4 %copy-start.23 = (bf16[640,768]{1,0:T(8,128)(2,1)S(1)}, bf16[640,768]{1,0:T(8,128)(2,1)}, u32[]{:S(2)}) copy-start(bf16[640,768]{1,0:T(8,128)(2,1)} %gather_fusion.2) | copy-start | bytes 2949124
  204.3 56.2 %slice-start = ((s8[9437184]{0:T(1024)(128)(4,1)}), s8[4194304]{0:T(1024)(128)(4,1)S(1)}, s32[]{:S(2)}) async-start(s8[9437184]{0:T(1024)(128)(4,1)} %bitcast.219), calls=%async_computation.20 | async-start | bytes 8388608
  204.3 56.2 %slice-start.1 = ((s8[9437184]{0:T(1024)(128)(4,1)}), s8[4194304]{0:T(1024)(128)(4,1)S(1)}, s32[]{:S(2)}) async-start(s8[9437184]{0:T(1024)(128)(4,1)} %bitcast.219), calls=%async_computation.21 | async-start | bytes 8388608
  227.7 22.7 %copy-start.27 = (bf16[640,768]{1,0:T(8,128)(2,1)S(1)}, bf16[640,768]{1,0:T(8,128)(2,1)}, u32[]{:S(2)}) copy-start(bf16[640,768]{1,0:T(8,128)(2,1)} %gather_fusion.6) | copy-start | bytes 2949124
  227.7 22.7 %copy-start.65 = (pred[640]{0:T(1024)(128)(4,1)S(1)}, pred[640]{0:T(1024)(128)(4,1)}, u32[]{:S(2)}) copy-start(pred[640]{0:T(1024)(128)(4,1)} %broadcast_compare_fusion.3) | copy-start | bytes 1924
  227.7 32.8 %slice-start.2 = ((s8[9437184]{0:T(1024)(128)(4,1)}), s8[1048576]{0:T(1024)(128)(4,1)S(1)}, s32[]{:S(2)}) async-start(s8[9437184]{0:T(1024)(128)(4,1)} %bitcast.219), calls=%async_computation.22 | async-start | bytes 2097152
  260.5 4.6 copy-start.20
  291.2 11.7 copy-start.36
  291.2 11.7 copy-start.40
  291.2 11.7 copy-start.42
  291.2 11.7 copy-start.44
  302.9 5.2 copy-start.50
  302.9 5.2 copy-start.3
  302.9 5.2 copy-start.9
  302.9 5.3 copy-start.60
  317.6 24.7 %all-to-all-start.1 = ((bf16[8,128,768]{1,0,2:T(8,128)(2,1)}), bf16[8,128,768]{1,0,2:T(8,128)(2,1)}, u32[]{:S(2)}, u32[]{:S(2)}) async-start(bf16[8,128,768]{1,0,2:T(8,128)(2,1)} %copy.86), calls=%async_computation.1 | async-start | bytes 3145728 | tf_op jit(solution)/shard_map/all_to_all | solution.py:176
  322.0 287.5 %reduce-scatter.19.cloned.1.call-start = ((), (), s32[]{:S(2)}) async-start(), calls=%async_computation.12 | async-start | bytes 2654208 | tf_op jit(solution)/shard_map/reduce_scatter | solution.py:211
  350.2 20.0 %copy-start.7 = (pred[8,512,512]{1,2,0:T(8,128)(4,1)S(1)}, pred[8,512,512]{1,2,0:T(8,128)(4,1)}, u32[]{:S(2)}) copy-start(pred[8,512,512]{1,2,0:T(8,128)(4,1)} %broadcast_compare_fusion) | copy-start | bytes 6291460
  350.2 20.0 %copy-start.31 = (f32[8,3,512]{2,1,0:T(4,128)S(1)}, f32[8,3,512]{2,1,0:T(4,128)}, u32[]{:S(2)}) copy-start(f32[8,3,512]{2,1,0:T(4,128)} %log_add_fusion) | copy-start | bytes 147460
  370.2 22.2 %copy-start.13 = (bf16[8,512,1,192]{1,3,2,0:T(8,128)(2,1)S(1)}, bf16[8,512,1,192]{1,3,2,0:T(8,128)(2,1)}, u32[]{:S(2)}) copy-start(bf16[8,512,1,192]{1,3,2,0:T(8,128)(2,1)} %copy-done.12) | copy-start | bytes 4718596
  387.8 4.6 copy-start.4
  395.7 9.8 copy-start.18
  438.7 5.3 copy-start.2
  438.7 5.3 copy-start.38
  438.7 5.4 copy-start.46
  438.7 5.4 copy-start.48
  438.7 75.9 %all-to-all-start.2 = ((bf16[8,512,3,192]{3,0,2,1:T(8,128)(2,1)}), bf16[8,512,3,192]{3,0,2,1:T(8,128)(2,1)}, u32[]{:S(2)}, u32[]{:S(2)}) async-start(bf16[8,512,3,192]{3,0,2,1:T(8,128)(2,1)} %pad_maximum_fusion.2), calls=%async_computation.2 | async-start | bytes 12582912 | tf_op jit(solution)/shard_map/all_to_all | solution.py:198
  443.9 222.9 %reduce-scatter.17.cloned.1.call-start = ((), (), s32[]{:S(2)}) async-start(), calls=%async_computation.11 | async-start | bytes 7962624 | tf_op jit(solution)/shard_map/reduce_scatter | solution.py:210
  523.2 7.7 copy-start.26
  536.8 442.8 %reduce-scatter.21.cloned.1.call-start = ((), (), s32[]{:S(2)}) async-start(), calls=%async_computation.13 | async-start | bytes 21233664 | tf_op jit(solution)/shard_map/reduce_scatter | solution.py:214
  537.0 6.5 copy-start.22
  537.0 6.5 copy-start.24
  554.4 737.7 %reduce-scatter.23.cloned.1.call-start = ((), (), s32[]{:S(2)}) async-start(), calls=%async_computation.14 | async-start | bytes 21233664 | tf_op jit(solution)/shard_map/reduce_scatter | solution.py:215
  555.0 6.5 copy-start.29
  555.0 6.5 copy-start.68
  555.0 6.5 copy-start.72
  572.5 9.7 copy-start.53
  572.6 783.9 %reduce-scatter.31.cloned.1.call-start = ((), (), s32[]{:S(2)}) async-start(), calls=%async_computation.18 | async-start | bytes 442368
  578.7 842.1 %reduce-scatter.29.cloned.1.call-start = ((), (), s32[]{:S(2)}) async-start(), calls=%async_computation.17 | async-start | bytes 442368
  581.7 903.6 %reduce-scatter.27.cloned.1.call-start = ((), (), s32[]{:S(2)}) async-start(), calls=%async_computation.16 | async-start | bytes 442368
  598.1 951.9 %reduce-scatter.25.cloned.1.call-start = ((), (), s32[]{:S(2)}) async-start(), calls=%async_computation.15 | async-start | bytes 442368
  601.1 1016.4 %all-reduce.4.cloned.1.call-start = ((), (), s32[]{:S(2)}) async-start(), calls=%async_computation.19 | async-start | bytes 5898240 | tf_op jit(solution)/shard_map/psum | solution.py:220
  1426.8 124.0 %copy-start.69 = (bf16[2,96]{1,0:T(2,128)(2,1)S(1)}, bf16[2,96]{1,0:T(2,128)(2,1)}, u32[]{:S(2)}) copy-start(bf16[2,96]{1,0:T(2,128)(2,1)} %copy.111) | copy-start | bytes 1156
  1426.9 124.0 %copy-start.70 = (bf16[2,96]{1,0:T(2,128)(2,1)S(1)}, bf16[2,96]{1,0:T(2,128)(2,1)}, u32[]{:S(2)}) copy-start(bf16[2,96]{1,0:T(2,128)(2,1)} %copy.109) | copy-start | bytes 1156
  1617.5 5.8 copy-start.32
  1617.5 6.8 copy-start.34
  (27 other events, 57.8 us)
Sparse Core Ops, SparseCore 0:
  328.9 72.0 reduce-scatter.18
  536.9 129.9 reduce-scatter.16
  670.7 308.7 reduce-scatter.20
  983.3 308.7 reduce-scatter.22
  1295.2 61.2 reduce-scatter.30
  1359.6 61.1 reduce-scatter.28
  1424.1 61.1 reduce-scatter.26
  1488.6 61.2 reduce-scatter.24
  1553.1 64.3 all-reduce.3
